TPU v7x, 32 devices: a whole 2x2x4 slice. The times are simulated.
32 devices in a mesh: grp: 2 (over y), frm: 8 (over z, x), tp: 2 (over core).
Axes of the slice: x: 2, y: 2, z: 4, core: 2. Of those that a mesh axis runs over, the one named last changes fastest.
Arguments:
- queries: bfloat16 [3072, 2560], P(('grp', 'frm'), 'tp'), parts along dimension 0, may hold values from -60 to 60, as said below
- key_rows: bfloat16 [3072, 2560], P(('grp', 'frm'), 'tp'), parts along dimension 0, may hold values from -60 to 60
- values: bfloat16 [3072, 2560], P(('grp', 'frm'), 'tp'), parts along dimension 0, may hold values from -6 to 6
- query_gain: float32 [2560], P('tp'), may hold values from 0.25 to 1.75
- key_gain: float32 [2560], P('tp'), may hold values from 0.25 to 1.75
- pattern: int32 [16, 4], P(('grp', 'frm')), parts along dimension 0, may hold values 0 or 1
- reference_keys: bfloat16 [64, 2560], P(('grp', 'frm'), 'tp'), parts along dimension 0, may hold values from -6 to 6
- reference_values: bfloat16 [64, 2560], P(('grp', 'frm'), 'tp'), parts along dimension 0, may hold values from -6 to 6
- reference_live: int32 [16], P(('grp', 'frm')), parts along dimension 0, may hold values from 1 to 4
Outputs:
- attention: bfloat16 [3072, 2560], P(('grp', 'frm'), 'tp'), parts along dimension 0
There are 2 independent parts, one for each index of `grp`. A program takes and returns all parts, laid end to end along the dimension named above; an argument that names none is the same for every part. Nothing has to cross between parts.
Inputs may be any that keep to these rules, and one draw needn't show every extreme that they name: `queries`: query entries lie within the range.
All inputs are finite; a program needn't handle non-finite values. No bound on the sum of `pattern` on one device may be relied on, other than what follows from the above.
Results may differ from a plain program's by a relative error of at most 0.012.
The roundings to bfloat16 on the way count: a program that leaves them out, or rounds other values in their place, can miss the bound.
Values may be sent and summed in bfloat16 or wider, within the bound.
No kernel may reach another device: no remote copies, remote signals or barrier semaphores. Data moves between devices by JAX's collectives and lax.ppermute only.
A program may use at most 64 MiB of HBM per device.

v0:
```python
import jax
import jax.numpy as jnp
from jax import lax
from jax.sharding import PartitionSpec as P

HEADS = 20
HEAD_DIM = 128
WINDOW = 2
EPSILON = 1e-06
NEG_FLOOR = -1e30


def passed_along(block, axis, distance):
    devices = range(lax.axis_size(axis))
    route = [((i - distance) % len(devices), i) for i in devices]
    return lax.ppermute(block, axis, route)


def normalize(matrix, scaling, square_sum, features):
    widened = matrix.astype(jnp.float32)
    return (widened * lax.rsqrt(square_sum / features + EPSILON)[:, None] * scaling).astype(
        jnp.bfloat16
    )


def absorb(state, query_part, key_part, value_part, allowed):
    running_max, running_sum, numerator = state
    scaling = query_part.shape[2] ** (-0.5)
    scores = (
        jnp.einsum("thd,nhd->htn", query_part, key_part, preferred_element_type=jnp.float32)
        * scaling
    )
    scores = jnp.where(allowed[None, None, :], scores, -jnp.inf)
    new_max = jnp.maximum(running_max, jnp.max(scores, axis=2))
    weights = jnp.exp(scores - new_max[:, :, None])
    fading = jnp.exp(running_max - new_max)
    running_sum = running_sum * fading + jnp.sum(weights, axis=2)
    numerator = numerator * jnp.transpose(fading)[:, :, None] + jnp.einsum(
        "htn,nhd->thd", weights.astype(jnp.bfloat16), value_part, preferred_element_type=jnp.float32
    )
    return (new_max, running_sum, numerator)


def attend(state, query_heads, key_heads, value_heads, allowed):
    group_width = query_heads.shape[1] // len(state)
    updated = []
    for group_id, group_state in enumerate(state):
        first_head = group_id * group_width
        last_head = first_head + group_width
        updated.append(
            absorb(
                group_state,
                query_heads[:, first_head:last_head],
                key_heads[:, first_head:last_head],
                value_heads[:, first_head:last_head],
                allowed,
            )
        )
    return tuple(updated)


def shards(
    queries,
    key_rows,
    values,
    query_gain,
    key_gain,
    pattern,
    reference_keys,
    reference_values,
    reference_live,
):
    tokens_here, features = queries.shape
    heads_here = features // HEAD_DIM
    squares = lax.psum(
        (
            jnp.sum(jnp.square(queries.astype(jnp.float32)), axis=1),
            jnp.sum(jnp.square(key_rows.astype(jnp.float32)), axis=1),
        ),
        "tp",
    )
    full_width = HEADS * HEAD_DIM
    normed_queries = normalize(queries, query_gain, squares[0], full_width)
    normed_keys = normalize(key_rows, key_gain, squares[1], full_width)
    query_heads = normed_queries.reshape(tokens_here, heads_here, HEAD_DIM)
    own_pair = jnp.stack([normed_keys, values])
    offsets = [column - WINDOW for column in range(WINDOW)] + [
        column + 1 for column in range(WINDOW)
    ]
    arrived = [passed_along(own_pair, "frm", -offset) for offset in offsets]
    groups = 2
    group_width = heads_here // groups
    start_state = tuple(
        (
            (
                jnp.full((group_width, tokens_here), NEG_FLOOR, jnp.float32),
                jnp.zeros((group_width, tokens_here), jnp.float32),
                jnp.zeros((tokens_here, group_width, HEAD_DIM), jnp.float32),
            )
            for group_id in range(groups)
        )
    )
    near_live = pattern[0] > 0

    def split_heads(matrix):
        return matrix.reshape(matrix.shape[0], heads_here, HEAD_DIM)

    every_pair = [own_pair] + arrived
    all_keys = split_heads(jnp.concatenate([key_value[0] for key_value in every_pair], axis=0))
    all_values = split_heads(jnp.concatenate([key_value[1] for key_value in every_pair], axis=0))
    flags = jnp.concatenate([jnp.ones((1,), jnp.bool_), near_live])
    allowed = jnp.repeat(flags, tokens_here)
    row_flags = (jnp.arange(reference_keys.shape[0], dtype=jnp.int32) < reference_live[0]).astype(
        jnp.bfloat16
    )
    pieces = (
        lax.all_gather(reference_keys, "frm", axis=0, tiled=True),
        lax.all_gather(reference_values, "frm", axis=0, tiled=True),
        lax.all_gather(row_flags, "frm", axis=0, tiled=True),
    )
    row_count = pieces[0].shape[0]
    final_state = attend(
        attend(start_state, query_heads, all_keys, all_values, allowed),
        query_heads,
        pieces[0].reshape(row_count, heads_here, HEAD_DIM),
        pieces[1].reshape(row_count, heads_here, HEAD_DIM),
        pieces[2] > 0.5,
    )
    outputs = [
        group_state[2] / jnp.transpose(group_state[1])[:, :, None] for group_state in final_state
    ]
    return jnp.concatenate(outputs, axis=1).reshape(tokens_here, features).astype(jnp.bfloat16)


def solution(mesh):
    in_specs = (
        P(("grp", "frm"), "tp"),
        P(("grp", "frm"), "tp"),
        P(("grp", "frm"), "tp"),
        P("tp"),
        P("tp"),
        P(("grp", "frm"), None),
        P(("grp", "frm"), "tp"),
        P(("grp", "frm"), "tp"),
        P(("grp", "frm")),
    )
    out_specs = P(("grp", "frm"), "tp")
    return jax.shard_map(shards, mesh=mesh, in_specs=in_specs, out_specs=out_specs, check_vma=False)
```

profile of v0, /device:TPU:0, one launch (start us, length us, event | category | flops | bytes accessed | tf_op | source)
XLA Modules:
  0.0 187.1 jit_solution(17618880381193820832)
XLA Ops:
  0.0 1.3 fusion.65
  1.3 1.2 fusion.62
  2.5 2.6 %all-reduce.1 = (f32[192]{0:T(256)S(1)}, f32[192]{0:T(256)S(1)}) all-reduce(f32[192]{0:T(256)S(1)} %fusion.65, f32[192]{0:T(256)S(1)} %fusion.62), channel_id=1, replica_groups=mesh['grp'=2,'frm'=8,'tp'=2] {'tp'}, use_global_device_ids=true, to_apply=%region_3.0 | all-reduce | flops 384 | bytes 3072 | tf_op jit(solution)/shard_map/psum | solution.py:75
  5.1 1.2 fusion.108
  6.3 2.1 %pad_maximum_fusion = bf16[2,192,1280]{2,1,0:T(8,128)(2,1)} fusion(bf16[1,192,1280]{2,1,0:T(8,128)(2,1)} %bitcast.111, bf16[1,192,1280]{2,1,0:T(8,128)(2,1)S(1)} %fusion.108), kind=kLoop, calls=%fused_computation.54 | loop fusion | flops 491520 | bytes 1966080 | tf_op jit(solution)/shard_map/stack | solution.py:86
  8.4 2.9 %collective-permute-start = (bf16[2,192,1280]{2,1,0:T(8,128)(2,1)}, bf16[2,192,1280]{2,1,0:T(8,128)(2,1)}, u32[]{:S(2)}, u32[]{:S(2)}) collective-permute-start(bf16[2,192,1280]{2,1,0:T(8,128)(2,1)} %pad_maximum_fusion), channel_id=1, source_target_pairs={{12,0},{14,2},{0,4},{2,6},{4,8},{6,10},{8,12},{10,14},{13,1},{15,3... | collective-permute-start | bytes 2949128 | tf_op jit(solution)/shard_map/ppermute | solution.py:16
  11.4 1.5 collective-permute-start.1
  12.8 3.2 %collective-permute-start.2 = (bf16[2,192,1280]{2,1,0:T(8,128)(2,1)}, bf16[2,192,1280]{2,1,0:T(8,128)(2,1)S(1)}, u32[]{:S(2)}, u32[]{:S(2)}) collective-permute-start(bf16[2,192,1280]{2,1,0:T(8,128)(2,1)} %pad_maximum_fusion), channel_id=1, source_target_pairs={{2,0},{4,2},{6,4},{8,6},{10,8},{12,10},{14,12},{0,14},{3,1},{5,3},... | collective-permute-start | bytes 2949128 | tf_op jit(solution)/shard_map/ppermute | solution.py:16
  16.1 0.3 collective-permute-start.3
  16.8 0.3 copy.56
  17.1 0.9 constant_dynamic-update-slice_fusion.9
  19.0 0.3 copy.46
  19.3 0.9 constant_dynamic-update-slice_fusion.4
  20.2 82.3 %all-gather = bf16[8,4,1280]{2,1,0:T(4,128)(2,1)S(1)} all-gather(bf16[1,4,1280]{2,1,0:T(4,128)(2,1)S(1)} %bitcast.112), channel_id=1, replica_groups=mesh['grp'=2,'frm'=8,'tp'=2] {'frm'}, dimensions={0}, use_global_device_ids=true | all-gather | bytes 92160 | tf_op jit(solution)/shard_map/all_gather | solution.py:117
  103.1 0.6 dynamic-slice
  104.7 18.7 %all-reduce = bf16[32]{0:T(256)(128)(2,1)S(1)} all-reduce(bf16[32]{0:T(256)(128)(2,1)S(1)} %dynamic-update-slice), channel_id=1, replica_groups=mesh['grp'=2,'frm'=8,'tp'=2] {'frm'}, use_global_device_ids=true, to_apply=%add | all-reduce | flops 32 | bytes 128
  123.4 30.7 %all-gather.1 = bf16[8,4,1280]{2,1,0:T(4,128)(2,1)S(1)} all-gather(bf16[1,4,1280]{2,1,0:T(4,128)(2,1)S(1)} %bitcast.113), channel_id=1, replica_groups=mesh['grp'=2,'frm'=8,'tp'=2] {'frm'}, dimensions={0}, use_global_device_ids=true | all-gather | bytes 92160 | tf_op jit(solution)/shard_map/all_gather | solution.py:118
  154.4 0.6 fusion.100
  155.1 0.8 fusion.102
  155.9 2.0 %fusion.99 = (bf16[1,192,1280]{2,1,0:T(8,128)(2,1)}, bf16[1,192,1280]{2,1,0:T(8,128)(2,1)S(1)}) fusion(bf16[2,192,1280]{2,1,0:T(8,128)(2,1)} %collective-permute-done), kind=kLoop, calls=%fused_computation.111 | loop fusion | bytes 1966080 | tf_op jit(solution)/shard_map/slice | solution.py:109
  158.2 0.3 copy.57
  158.5 2.0 %fusion.98 = (bf16[1,192,1280]{2,1,0:T(8,128)(2,1)}, bf16[1,192,1280]{2,1,0:T(8,128)(2,1)S(1)}) fusion(bf16[2,192,1280]{2,1,0:T(8,128)(2,1)} %collective-permute-done.1), kind=kLoop, calls=%fused_computation.110 | loop fusion | bytes 1966080 | tf_op jit(solution)/shard_map/slice | solution.py:109
  160.8 0.3 copy.58
  161.1 0.9 fusion.97
  162.2 0.3 copy.59
  162.5 2.0 %fusion.96 = (bf16[1,192,1280]{2,1,0:T(8,128)(2,1)}, bf16[1,192,1280]{2,1,0:T(8,128)(2,1)S(1)}) fusion(bf16[2,192,1280]{2,1,0:T(8,128)(2,1)} %collective-permute-done.3), kind=kLoop, calls=%fused_computation.108 | loop fusion | bytes 1966080 | tf_op jit(solution)/shard_map/slice | solution.py:109
  164.8 0.3 copy.60
  165.1 1.3 copy.42
  166.4 1.0 copy.47
  167.4 1.3 copy.43
  168.7 1.0 copy.48
  169.7 1.3 copy.44
  170.9 1.1 copy.49
  172.0 1.3 copy.45
  173.3 1.0 copy.50
  174.3 0.9 constant_dynamic-update-slice_fusion.8
  175.2 0.9 constant_dynamic-update-slice_fusion.7
  176.1 0.9 constant_dynamic-update-slice_fusion.6
  177.0 0.9 constant_dynamic-update-slice_fusion.5
  178.2 1.1 fusion
  179.3 1.9 %fusion.2 = (f32[5,192]{1,0:T(8,128)S(1)}, f32[5,192]{1,0:T(8,128)S(1)}, f32[5,192,960]{2,1,0:T(8,128)S(1)}) fusion(f32[5,192,960]{2,1,0:T(8,128)S(1)} %get-tuple-element.36, f32[5,192]{1,0:T(8,128)S(1)} %get-tuple-element.27, pred[960]{0:T(1024)(128)(4,1)S(1)} %broadcast_in_dim.54, bf16[192,10,128]{0,2,1:T(8,128)(2,1)S(1)} %bitcast.99, ...), kind=kOutput, calls=%fused_computation.6 | convolution fusion | flops 242378880 | bytes 9519616 | tf_op jit(solution)/shard_map/thd,nhd->htn/dot_general | solution.py:30
  181.3 1.0 fusion.4
  182.4 0.5 copy-done.8
  182.9 1.1 fusion.53
  184.0 1.1 fusion.48
  185.1 0.3 fusion.59
  185.5 0.3 fusion.58
  186.1 1.0 copy.67
  (71 shorter events, 3.7 us)
Async XLA Ops:
  0.0 16.6 %copy-start = (bf16[192,1280]{1,0:T(8,128)(2,1)S(1)}, bf16[192,1280]{1,0:T(8,128)(2,1)}, u32[]{:S(2)}) copy-start(bf16[192,1280]{1,0:T(8,128)(2,1)} %param.10) | copy-start | bytes 1474564
  0.0 16.6 %copy-start.11 = (f32[1280]{0:T(1024)S(1)}, f32[1280]{0:T(1024)}, u32[]{:S(2)}) copy-start(f32[1280]{0:T(1024)} %param.13) | copy-start | bytes 15364
  0.0 16.4 %copy-start.6 = (bf16[192,1280]{1,0:T(8,128)(2,1)S(1)}, bf16[192,1280]{1,0:T(8,128)(2,1)}, u32[]{:S(2)}) copy-start(bf16[192,1280]{1,0:T(8,128)(2,1)} %param.11) | copy-start | bytes 1474564
  8.4 9.6 %copy-start.15 = (s32[1,4]{1,0:T(1,128)S(1)}, s32[1,4]{1,0:T(1,128)}, u32[]{:S(2)}) copy-start(s32[1,4]{1,0:T(1,128)} %param.14) | copy-start | bytes 52
  8.4 9.9 %copy-start.1 = (bf16[192,1280]{1,0:T(8,128)(2,1)S(1)}, bf16[192,1280]{1,0:T(8,128)(2,1)}, u32[]{:S(2)}) copy-start(bf16[192,1280]{1,0:T(8,128)(2,1)} %param.9) | copy-start | bytes 1474564
  8.4 9.9 %copy-start.14 = (f32[1280]{0:T(1024)S(1)}, f32[1280]{0:T(1024)}, u32[]{:S(2)}) copy-start(f32[1280]{0:T(1024)} %param.12) | copy-start | bytes 15364
  8.4 147.5 %collective-permute-start = (bf16[2,192,1280]{2,1,0:T(8,128)(2,1)}, bf16[2,192,1280]{2,1,0:T(8,128)(2,1)}, u32[]{:S(2)}, u32[]{:S(2)}) collective-permute-start(bf16[2,192,1280]{2,1,0:T(8,128)(2,1)} %pad_maximum_fusion), channel_id=1, source_target_pairs={{12,0},{14,2},{0,4},{2,6},{4,8},{6,10},{8,12},{10,14},{13,1},{15,3... | collective-permute-start | bytes 2949128 | tf_op jit(solution)/shard_map/ppermute | solution.py:16
  11.4 147.2 %collective-permute-start.1 = (bf16[2,192,1280]{2,1,0:T(8,128)(2,1)}, bf16[2,192,1280]{2,1,0:T(8,128)(2,1)}, u32[]{:S(2)}, u32[]{:S(2)}) collective-permute-start(bf16[2,192,1280]{2,1,0:T(8,128)(2,1)} %pad_maximum_fusion), channel_id=1, source_target_pairs={{14,0},{0,2},{2,4},{4,6},{6,8},{8,10},{10,12},{12,14},{15,1},{1,3}... | collective-permute-start | bytes 2949128 | tf_op jit(solution)/shard_map/ppermute | solution.py:16
  12.8 148.3 %collective-permute-start.2 = (bf16[2,192,1280]{2,1,0:T(8,128)(2,1)}, bf16[2,192,1280]{2,1,0:T(8,128)(2,1)S(1)}, u32[]{:S(2)}, u32[]{:S(2)}) collective-permute-start(bf16[2,192,1280]{2,1,0:T(8,128)(2,1)} %pad_maximum_fusion), channel_id=1, source_target_pairs={{2,0},{4,2},{6,4},{8,6},{10,8},{12,10},{14,12},{0,14},{3,1},{5,3},... | collective-permute-start | bytes 2949128 | tf_op jit(solution)/shard_map/ppermute | solution.py:16
  16.1 146.5 %collective-permute-start.3 = (bf16[2,192,1280]{2,1,0:T(8,128)(2,1)}, bf16[2,192,1280]{2,1,0:T(8,128)(2,1)}, u32[]{:S(2)}, u32[]{:S(2)}) collective-permute-start(bf16[2,192,1280]{2,1,0:T(8,128)(2,1)} %pad_maximum_fusion), channel_id=1, source_target_pairs={{4,0},{6,2},{8,4},{10,6},{12,8},{14,10},{0,12},{2,14},{5,1},{7,3},... | collective-permute-start | bytes 2949128 | tf_op jit(solution)/shard_map/ppermute | solution.py:16
  18.5 1.7 copy-start.12
  18.5 84.6 %copy-start.16 = (u32[32]{0:T(128)S(1)}, u32[32]{0:T(128)}, u32[]{:S(2)}) copy-start(u32[32]{0:T(128)} %constant.29) | copy-start | bytes 388
  18.5 104.9 %copy-start.13 = (bf16[4,1280]{1,0:T(4,128)(2,1)S(1)}, bf16[4,1280]{1,0:T(4,128)(2,1)}, u32[]{:S(2)}) copy-start(bf16[4,1280]{1,0:T(4,128)(2,1)} %param.16) | copy-start | bytes 30724
  174.3 3.6 %copy-start.2 = (bf16[192,10,128]{2,0,1:T(8,128)(2,1)S(1)}, bf16[192,10,128]{2,0,1:T(8,128)(2,1)}, u32[]{:S(2)}) copy-start(bf16[192,10,128]{2,0,1:T(8,128)(2,1)} %copy.47) | copy-start | bytes 1474564
  174.3 3.6 %copy-start.9 = (bf16[960,10,128]{2,0,1:T(8,128)(2,1)S(1)}, bf16[960,10,128]{2,0,1:T(8,128)(2,1)}, u32[]{:S(2)}) copy-start(bf16[960,10,128]{2,0,1:T(8,128)(2,1)} %constant_dynamic-update-slice_fusion.4) | copy-start | bytes 7372804
  174.3 3.7 %copy-start.3 = (bf16[192,10,128]{2,0,1:T(8,128)(2,1)S(1)}, bf16[192,10,128]{2,0,1:T(8,128)(2,1)}, u32[]{:S(2)}) copy-start(bf16[192,10,128]{2,0,1:T(8,128)(2,1)} %copy.48) | copy-start | bytes 1474564
  175.2 2.9 %copy-start.4 = (bf16[192,10,128]{2,0,1:T(8,128)(2,1)S(1)}, bf16[192,10,128]{2,0,1:T(8,128)(2,1)}, u32[]{:S(2)}) copy-start(bf16[192,10,128]{2,0,1:T(8,128)(2,1)} %copy.49) | copy-start | bytes 1474564
  176.1 2.0 %copy-start.5 = (bf16[192,10,128]{2,0,1:T(8,128)(2,1)S(1)}, bf16[192,10,128]{2,0,1:T(8,128)(2,1)}, u32[]{:S(2)}) copy-start(bf16[192,10,128]{2,0,1:T(8,128)(2,1)} %copy.50) | copy-start | bytes 1474564
  179.3 1.9 %copy-start.7 = (f32[5,192,32]{1,2,0:T(8,128)S(1)}, f32[5,192,32]{1,2,0:T(8,128)}, u32[]{:S(2)}) copy-start(f32[5,192,32]{1,2,0:T(8,128)} %get-tuple-element.32) | copy-start | bytes 368644
  181.2 1.7 copy-start.8
  184.0 1.1 copy-start.10
where the time goes:
time: 188 us; the launch traced here: 187 us
  blocking collectives  134 us (71%)
  local copies, waits for them, and re-layouts  28.9 us (15%)
  starting transfers between devices  7.92 us (4%)
  other arithmetic  7.48 us (4%)
  matrix products  6.85 us (4%)
    all_gather x1, blocking collectives, shards(): lax.all_gather(reference_keys, 'frm', axis=0, tiled=True)  82.3 us
    all_gather x1, blocking collectives, shards(): lax.all_gather(reference_values, 'frm', axis=0, tiled=True)  30.7 us
    unnamed x1, blocking collectives  18.7 us
    slice x8, local copies, waits for them, and re-layouts, shards(): key_value[0]  12 us
    ppermute x4, starting transfers between devices, passed_along(): return lax.ppermute(block, axis, route)  7.92 us
    unnamed x46, local copies, waits for them, and re-layouts  6.38 us
    concatenate x6, local copies, waits for them, and re-layouts, shards(): jnp.concatenate([key_value[0] for key_value in every_pair], axis=0)  4.48 us
    dot_general x4, matrix products, absorb(): jnp.einsum('thd,nhd->htn', query_part, key_part, preferred_element_type=j...  4 us
  transfers between devices with their start and end apart: 4, of which 0 were waited for; matrix products, arithmetic and copies ran while one was open for 7% of the time, Pallas kernels for 0%

commit v1 on v0

--- a/solution.py
+++ b/solution.py
@@ -8,6 +8,21 @@
 WINDOW = 2
 EPSILON = 1e-06
 NEG_FLOOR = -1e30
+
+
+def order_entries(dim_k, my_data):
+    across = "frm"
+    left_arr, k_now = (lax.axis_size(across), lax.axis_index(across))
+    heard, t1 = (my_data, 1)
+    while t1 < left_arr:
+        val = lax.ppermute(
+            heard, axis_name=across, perm=list(map(lambda k0: (k0, k0 ^ t1), range(left_arr)))
+        )
+        everything = jnp.concatenate([heard, val], axis=dim_k)
+        piece_out = jnp.concatenate([val, heard], axis=dim_k)
+        heard = jnp.where(k_now & t1 == 0, everything, piece_out)
+        t1 = 2 * t1
+    return heard
 
 
 def passed_along(block, axis, distance):
@@ -115,7 +130,7 @@
     )
     pieces = (
         lax.all_gather(reference_keys, "frm", axis=0, tiled=True),
-        lax.all_gather(reference_values, "frm", axis=0, tiled=True),
+        order_entries(0, reference_values),
         lax.all_gather(row_flags, "frm", axis=0, tiled=True),
     )
     row_count = pieces[0].shape[0]

time: 188 us -> 166 us (0.88)
  blocking collectives: 134 us -> 104 us
  waiting for transfers between devices: 0.01 us -> 8.62 us
    all_gather x1 -> x0, blocking collectives: 30.7 us -> none  [shards(): lax.all_gather(reference_values, 'frm', axis=0, tiled=True)]
    ppermute x0 -> x3, waiting for transfers between devices: none -> 8.61 us  [order_entries(): lax.ppermute(heard, axis_name=across, perm=list(map(lambda k0: (k0, k0 ^...]
    unnamed x46 -> x44, local copies, waits for them, and re-layouts: 6.38 us -> 6.28 us
  transfers between devices with their start and end apart: 4 -> 7, of which waited for: 0 -> 2; matrix products, arithmetic and copies ran while one was open for 7% -> 7% of each run, Pallas kernels for 0% -> 0%
where the time goes in v1:
time: 166 us; the launch traced here: 165 us
  blocking collectives  104 us (63%)
  local copies, waits for them, and re-layouts  28.1 us (17%)
  starting transfers between devices  8.81 us (5%)
  waiting for transfers between devices  8.62 us (5%)
  other arithmetic  7.56 us (5%)
  matrix products  6.81 us (4%)
  between operations  1.76 us (1%)
    all_gather x1, blocking collectives, shards(): lax.all_gather(reference_keys, 'frm', axis=0, tiled=True)  82.2 us
    unnamed x1, blocking collectives  18.9 us
    slice x8, local copies, waits for them, and re-layouts, shards(): key_value[0]  12 us
    ppermute x3, waiting for transfers between devices, order_entries(): lax.ppermute(heard, axis_name=across, perm=list(map(lambda k0: (k0, k0 ^...  8.61 us
    ppermute x4, starting transfers between devices, passed_along(): return lax.ppermute(block, axis, route)  7.89 us
    unnamed x44, local copies, waits for them, and re-layouts  6.28 us
    concatenate x6, local copies, waits for them, and re-layouts, shards(): jnp.concatenate([key_value[0] for key_value in every_pair], axis=0)  4.49 us
    dot_general x4, matrix products, absorb(): jnp.einsum('thd,nhd->htn', query_part, key_part, preferred_element_type=j...  4 us
  transfers between devices with their start and end apart: 7, of which 2 were waited for; matrix products, arithmetic and copies ran while one was open for 7% of the time, Pallas kernels for 0%

profile of v1, /device:TPU:0, one launch (start us, length us, event | category | flops | bytes accessed | tf_op | source)
XLA Modules:
  0.0 165.4 jit_solution(15596802892050658033)
XLA Ops:
  0.0 1.3 fusion.65
  1.3 1.2 fusion.62
  2.5 2.6 %all-reduce.1 = (f32[192]{0:T(256)S(1)}, f32[192]{0:T(256)S(1)}) all-reduce(f32[192]{0:T(256)S(1)} %fusion.65, f32[192]{0:T(256)S(1)} %fusion.62), channel_id=1, replica_groups=mesh['grp'=2,'frm'=8,'tp'=2] {'tp'}, use_global_device_ids=true, to_apply=%region_3.0 | all-reduce | flops 384 | bytes 3072 | tf_op jit(solution)/shard_map/psum | solution.py:90
  5.1 1.2 fusion.107
  6.4 2.1 %pad_maximum_fusion = bf16[2,192,1280]{2,1,0:T(8,128)(2,1)} fusion(bf16[1,192,1280]{2,1,0:T(8,128)(2,1)} %bitcast.118, bf16[1,192,1280]{2,1,0:T(8,128)(2,1)S(1)} %fusion.107), kind=kLoop, calls=%fused_computation.54 | loop fusion | flops 491520 | bytes 1966080 | tf_op jit(solution)/shard_map/stack | solution.py:101
  8.5 2.9 %collective-permute-start = (bf16[2,192,1280]{2,1,0:T(8,128)(2,1)}, bf16[2,192,1280]{2,1,0:T(8,128)(2,1)}, u32[]{:S(2)}, u32[]{:S(2)}) collective-permute-start(bf16[2,192,1280]{2,1,0:T(8,128)(2,1)} %pad_maximum_fusion), channel_id=1, source_target_pairs={{12,0},{14,2},{0,4},{2,6},{4,8},{6,10},{8,12},{10,14},{13,1},{15,3... | collective-permute-start | bytes 2949128 | tf_op jit(solution)/shard_map/ppermute | solution.py:31
  11.4 1.5 collective-permute-start.1
  12.9 3.2 %collective-permute-start.2 = (bf16[2,192,1280]{2,1,0:T(8,128)(2,1)}, bf16[2,192,1280]{2,1,0:T(8,128)(2,1)S(1)}, u32[]{:S(2)}, u32[]{:S(2)}) collective-permute-start(bf16[2,192,1280]{2,1,0:T(8,128)(2,1)} %pad_maximum_fusion), channel_id=1, source_target_pairs={{2,0},{4,2},{6,4},{8,6},{10,8},{12,10},{14,12},{0,14},{3,1},{5,3},... | collective-permute-start | bytes 2949128 | tf_op jit(solution)/shard_map/ppermute | solution.py:31
  16.3 0.8 collective-permute-start.4
  17.6 0.3 copy.56
  17.9 0.9 constant_dynamic-update-slice_fusion.9
  19.1 0.3 copy.46
  19.4 0.9 constant_dynamic-update-slice_fusion.4
  20.3 82.2 %all-gather = bf16[8,4,1280]{2,1,0:T(4,128)(2,1)S(1)} all-gather(bf16[1,4,1280]{2,1,0:T(4,128)(2,1)S(1)} %bitcast.122), channel_id=1, replica_groups=mesh['grp'=2,'frm'=8,'tp'=2] {'frm'}, dimensions={0}, use_global_device_ids=true | all-gather | bytes 92160 | tf_op jit(solution)/shard_map/all_gather | solution.py:132
  103.5 0.6 dynamic-slice
  105.2 18.9 %all-reduce = bf16[32]{0:T(256)(128)(2,1)S(1)} all-reduce(bf16[32]{0:T(256)(128)(2,1)S(1)} %dynamic-update-slice), channel_id=1, replica_groups=mesh['grp'=2,'frm'=8,'tp'=2] {'frm'}, use_global_device_ids=true, to_apply=%add | all-reduce | flops 32 | bytes 128
  124.3 0.8 fusion.101
  125.5 3.7 %collective-permute-done.5 = bf16[8,1280]{1,0:T(8,128)(2,1)S(1)} collective-permute-done((bf16[8,1280]{1,0:T(8,128)(2,1)S(1)}, bf16[8,1280]{1,0:T(8,128)(2,1)S(1)}, u32[]{:S(2)}, u32[]{:S(2)}) %collective-permute-start.5) | collective-permute-done | bytes 20512 | tf_op jit(solution)/shard_map/ppermute | solution.py:18
  129.4 4.9 %collective-permute-done.6 = bf16[16,1280]{1,0:T(8,128)(2,1)S(1)} collective-permute-done((bf16[16,1280]{1,0:T(8,128)(2,1)S(1)}, bf16[16,1280]{1,0:T(8,128)(2,1)S(1)}, u32[]{:S(2)}, u32[]{:S(2)}) %collective-permute-start.6) | collective-permute-done | bytes 40992 | tf_op jit(solution)/shard_map/ppermute | solution.py:18
  134.3 2.0 %fusion.99 = (bf16[1,192,1280]{2,1,0:T(8,128)(2,1)}, bf16[1,192,1280]{2,1,0:T(8,128)(2,1)S(1)}) fusion(bf16[2,192,1280]{2,1,0:T(8,128)(2,1)} %collective-permute-done), kind=kLoop, calls=%fused_computation.117 | loop fusion | bytes 1966080 | tf_op jit(solution)/shard_map/slice | solution.py:124
  136.5 0.3 copy.57
  136.8 2.1 %fusion.98 = (bf16[1,192,1280]{2,1,0:T(8,128)(2,1)}, bf16[1,192,1280]{2,1,0:T(8,128)(2,1)S(1)}) fusion(bf16[2,192,1280]{2,1,0:T(8,128)(2,1)} %collective-permute-done.1), kind=kLoop, calls=%fused_computation.116 | loop fusion | bytes 1966080 | tf_op jit(solution)/shard_map/slice | solution.py:124
  139.1 0.3 copy.58
  139.4 0.9 fusion.97
  140.5 0.3 copy.59
  140.9 2.0 %fusion.96 = (bf16[1,192,1280]{2,1,0:T(8,128)(2,1)}, bf16[1,192,1280]{2,1,0:T(8,128)(2,1)S(1)}) fusion(bf16[2,192,1280]{2,1,0:T(8,128)(2,1)} %collective-permute-done.3), kind=kLoop, calls=%fused_computation.114 | loop fusion | bytes 1966080 | tf_op jit(solution)/shard_map/slice | solution.py:124
  143.1 0.3 copy.60
  143.4 1.3 copy.42
  144.7 1.0 copy.47
  145.7 1.3 copy.43
  147.0 1.0 copy.48
  148.0 1.3 copy.44
  149.3 1.1 copy.49
  150.4 1.3 copy.45
  151.6 1.0 copy.50
  152.6 0.9 constant_dynamic-update-slice_fusion.8
  153.5 0.9 constant_dynamic-update-slice_fusion.7
  154.4 0.9 constant_dynamic-update-slice_fusion.6
  155.3 0.9 constant_dynamic-update-slice_fusion.5
  156.5 1.1 fusion
  157.6 1.9 %fusion.2 = (f32[5,192]{1,0:T(8,128)S(1)}, f32[5,192]{1,0:T(8,128)S(1)}, f32[5,192,960]{2,1,0:T(8,128)S(1)}) fusion(f32[5,192,960]{2,1,0:T(8,128)S(1)} %get-tuple-element.34, f32[5,192]{1,0:T(8,128)S(1)} %get-tuple-element.25, pred[960]{0:T(1024)(128)(4,1)S(1)} %broadcast_in_dim.54, bf16[192,10,128]{0,2,1:T(8,128)(2,1)S(1)} %bitcast.106, ...), kind=kOutput, calls=%fused_computation.6 | convolution fusion | flops 242378880 | bytes 9519616 | tf_op jit(solution)/shard_map/thd,nhd->htn/dot_general | solution.py:45
  159.6 1.0 fusion.4
  160.7 0.5 copy-done.9
  161.2 1.1 fusion.53
  162.3 1.1 fusion.48
  163.4 0.3 fusion.58
  163.7 0.3 fusion.59
  164.4 1.0 copy.67
  (77 shorter events, 4.1 us)
Async XLA Ops:
  0.0 17.4 %copy-start = (bf16[192,1280]{1,0:T(8,128)(2,1)S(1)}, bf16[192,1280]{1,0:T(8,128)(2,1)}, u32[]{:S(2)}) copy-start(bf16[192,1280]{1,0:T(8,128)(2,1)} %param.10) | copy-start | bytes 1474564
  0.0 17.4 %copy-start.11 = (f32[1280]{0:T(1024)S(1)}, f32[1280]{0:T(1024)}, u32[]{:S(2)}) copy-start(f32[1280]{0:T(1024)} %param.13) | copy-start | bytes 15364
  0.0 17.1 %copy-start.6 = (bf16[192,1280]{1,0:T(8,128)(2,1)S(1)}, bf16[192,1280]{1,0:T(8,128)(2,1)}, u32[]{:S(2)}) copy-start(bf16[192,1280]{1,0:T(8,128)(2,1)} %param.11) | copy-start | bytes 1474564
  0.0 16.3 %copy-start.10 = (bf16[4,1280]{1,0:T(4,128)(2,1)S(1)}, bf16[4,1280]{1,0:T(4,128)(2,1)}, u32[]{:S(2)}) copy-start(bf16[4,1280]{1,0:T(4,128)(2,1)} %param.16) | copy-start | bytes 30724
  8.4 10.4 %copy-start.14 = (s32[1,4]{1,0:T(1,128)S(1)}, s32[1,4]{1,0:T(1,128)}, u32[]{:S(2)}) copy-start(s32[1,4]{1,0:T(1,128)} %param.14) | copy-start | bytes 52
  8.5 125.8 %collective-permute-start = (bf16[2,192,1280]{2,1,0:T(8,128)(2,1)}, bf16[2,192,1280]{2,1,0:T(8,128)(2,1)}, u32[]{:S(2)}, u32[]{:S(2)}) collective-permute-start(bf16[2,192,1280]{2,1,0:T(8,128)(2,1)} %pad_maximum_fusion), channel_id=1, source_target_pairs={{12,0},{14,2},{0,4},{2,6},{4,8},{6,10},{8,12},{10,14},{13,1},{15,3... | collective-permute-start | bytes 2949128 | tf_op jit(solution)/shard_map/ppermute | solution.py:31
  11.4 125.5 %collective-permute-start.1 = (bf16[2,192,1280]{2,1,0:T(8,128)(2,1)}, bf16[2,192,1280]{2,1,0:T(8,128)(2,1)}, u32[]{:S(2)}, u32[]{:S(2)}) collective-permute-start(bf16[2,192,1280]{2,1,0:T(8,128)(2,1)} %pad_maximum_fusion), channel_id=1, source_target_pairs={{14,0},{0,2},{2,4},{4,6},{6,8},{8,10},{10,12},{12,14},{15,1},{1,3}... | collective-permute-start | bytes 2949128 | tf_op jit(solution)/shard_map/ppermute | solution.py:31
  12.9 126.6 %collective-permute-start.2 = (bf16[2,192,1280]{2,1,0:T(8,128)(2,1)}, bf16[2,192,1280]{2,1,0:T(8,128)(2,1)S(1)}, u32[]{:S(2)}, u32[]{:S(2)}) collective-permute-start(bf16[2,192,1280]{2,1,0:T(8,128)(2,1)} %pad_maximum_fusion), channel_id=1, source_target_pairs={{2,0},{4,2},{6,4},{8,6},{10,8},{12,10},{14,12},{0,14},{3,1},{5,3},... | collective-permute-start | bytes 2949128 | tf_op jit(solution)/shard_map/ppermute | solution.py:31
  16.1 124.8 %collective-permute-start.3 = (bf16[2,192,1280]{2,1,0:T(8,128)(2,1)}, bf16[2,192,1280]{2,1,0:T(8,128)(2,1)}, u32[]{:S(2)}, u32[]{:S(2)}) collective-permute-start(bf16[2,192,1280]{2,1,0:T(8,128)(2,1)} %pad_maximum_fusion), channel_id=1, source_target_pairs={{4,0},{6,2},{8,4},{10,6},{12,8},{14,10},{0,12},{2,14},{5,1},{7,3},... | collective-permute-start | bytes 2949128 | tf_op jit(solution)/shard_map/ppermute | solution.py:31
  16.3 109.0 %collective-permute-start.4 = (bf16[4,1280]{1,0:T(4,128)(2,1)S(1)}, bf16[4,1280]{1,0:T(4,128)(2,1)S(1)}, u32[]{:S(2)}, u32[]{:S(2)}) collective-permute-start(bf16[4,1280]{1,0:T(4,128)(2,1)S(1)} %copy-done.10), channel_id=1, source_target_pairs={{0,2},{2,0},{4,6},{6,4},{8,10},{10,8},{12,14},{14,12},{1,3},{3,1},... | collective-permute-start | bytes 30728 | tf_op jit(solution)/shard_map/ppermute | solution.py:18
  17.6 2.7 %copy-start.12 = (bf16[4,1280]{1,0:T(4,128)(2,1)S(1)}, bf16[4,1280]{1,0:T(4,128)(2,1)}, u32[]{:S(2)}) copy-start(bf16[4,1280]{1,0:T(4,128)(2,1)} %param.15) | copy-start | bytes 30724
  17.9 85.3 %copy-start.1 = (bf16[192,1280]{1,0:T(8,128)(2,1)S(1)}, bf16[192,1280]{1,0:T(8,128)(2,1)}, u32[]{:S(2)}) copy-start(bf16[192,1280]{1,0:T(8,128)(2,1)} %param.9) | copy-start | bytes 1474564
  17.9 85.3 %copy-start.13 = (f32[1280]{0:T(1024)S(1)}, f32[1280]{0:T(1024)}, u32[]{:S(2)}) copy-start(f32[1280]{0:T(1024)} %param.12) | copy-start | bytes 15364
  18.8 84.6 %copy-start.15 = (u32[32]{0:T(128)S(1)}, u32[32]{0:T(128)}, u32[]{:S(2)}) copy-start(u32[32]{0:T(128)} %constant.42) | copy-start | bytes 388
  125.4 3.8 %collective-permute-start.5 = (bf16[8,1280]{1,0:T(8,128)(2,1)S(1)}, bf16[8,1280]{1,0:T(8,128)(2,1)S(1)}, u32[]{:S(2)}, u32[]{:S(2)}) collective-permute-start(bf16[8,1280]{1,0:T(8,128)(2,1)S(1)} %maximum_select_fusion.4), channel_id=1, source_target_pairs={{0,4},{2,6},{4,0},{6,2},{8,12},{10,14},{12,8},{14,10},{1,5},{3,7},... | collective-permute-start | bytes 61448 | tf_op jit(solution)/shard_map/ppermute | solution.py:18
  129.3 5.0 %collective-permute-start.6 = (bf16[16,1280]{1,0:T(8,128)(2,1)S(1)}, bf16[16,1280]{1,0:T(8,128)(2,1)S(1)}, u32[]{:S(2)}, u32[]{:S(2)}) collective-permute-start(bf16[16,1280]{1,0:T(8,128)(2,1)S(1)} %maximum_select_fusion.2), channel_id=1, source_target_pairs={{0,8},{2,10},{4,12},{6,14},{8,0},{10,2},{12,4},{14,6},{1,9},{3,11}... | collective-permute-start | bytes 122888 | tf_op jit(solution)/shard_map/ppermute | solution.py:18
  152.6 3.6 %copy-start.2 = (bf16[192,10,128]{2,0,1:T(8,128)(2,1)S(1)}, bf16[192,10,128]{2,0,1:T(8,128)(2,1)}, u32[]{:S(2)}) copy-start(bf16[192,10,128]{2,0,1:T(8,128)(2,1)} %copy.47) | copy-start | bytes 1474564
  152.6 3.6 %copy-start.8 = (bf16[960,10,128]{2,0,1:T(8,128)(2,1)S(1)}, bf16[960,10,128]{2,0,1:T(8,128)(2,1)}, u32[]{:S(2)}) copy-start(bf16[960,10,128]{2,0,1:T(8,128)(2,1)} %constant_dynamic-update-slice_fusion.4) | copy-start | bytes 7372804
  152.6 3.6 %copy-start.3 = (bf16[192,10,128]{2,0,1:T(8,128)(2,1)S(1)}, bf16[192,10,128]{2,0,1:T(8,128)(2,1)}, u32[]{:S(2)}) copy-start(bf16[192,10,128]{2,0,1:T(8,128)(2,1)} %copy.48) | copy-start | bytes 1474564
  153.5 2.8 %copy-start.4 = (bf16[192,10,128]{2,0,1:T(8,128)(2,1)S(1)}, bf16[192,10,128]{2,0,1:T(8,128)(2,1)}, u32[]{:S(2)}) copy-start(bf16[192,10,128]{2,0,1:T(8,128)(2,1)} %copy.49) | copy-start | bytes 1474564
  154.4 2.0 %copy-start.5 = (bf16[192,10,128]{2,0,1:T(8,128)(2,1)S(1)}, bf16[192,10,128]{2,0,1:T(8,128)(2,1)}, u32[]{:S(2)}) copy-start(bf16[192,10,128]{2,0,1:T(8,128)(2,1)} %copy.50) | copy-start | bytes 1474564
  157.6 1.9 %copy-start.7 = (f32[5,192,32]{1,2,0:T(8,128)S(1)}, f32[5,192,32]{1,2,0:T(8,128)}, u32[]{:S(2)}) copy-start(f32[5,192,32]{1,2,0:T(8,128)} %get-tuple-element.30) | copy-start | bytes 368644
  159.5 1.7 %copy-start.9 = (bf16[960,10,128]{2,0,1:T(8,128)(2,1)S(1)}, bf16[960,10,128]{2,0,1:T(8,128)(2,1)}, u32[]{:S(2)}) copy-start(bf16[960,10,128]{2,0,1:T(8,128)(2,1)} %constant_dynamic-update-slice_fusion.5) | copy-start | bytes 7372804
